TPU v7x, 32 devices: a whole 2x2x4 slice. The times are simulated.
32 devices in a mesh: dp: 8 (over z, x), mp: 4 (over y, core).
Axes of the slice: x: 2, y: 2, z: 4, core: 2. Of those that a mesh axis runs over, the one named last changes fastest.
Arguments:
- tokens: bfloat16 [4096, 2048], P('dp'), may hold values from -6 to 6
- cotangent: bfloat16 [4096, 2048], P('dp'), may hold values from -6 to 6
- doc_ids: int32 [4096], P('dp'), may hold values from 0 to 1, as said below
- row_ids: int32 [8], P('dp'), may hold values from 0 to 2, as said below
- offsets: int32 [8], P('dp'), may hold values from 0 to 1536, as said below
- w_query: bfloat16 [2048, 2048], P(None, 'mp'), may hold values from -0.125 to 0.125
- w_key: bfloat16 [2048, 2048], P(None, 'mp'), may hold values from -0.125 to 0.125
- w_value: bfloat16 [2048, 2048], P(None, 'mp'), may hold values from -0.125 to 0.125
- w_output: bfloat16 [2048, 2048], P('mp'), may hold values from -0.125 to 0.125
- w_gate: bfloat16 [2048, 8192], P(None, 'mp'), may hold values from -0.125 to 0.125
- w_up: bfloat16 [2048, 8192], P(None, 'mp'), may hold values from -0.125 to 0.125
- w_down: bfloat16 [8192, 2048], P('mp'), may hold values from -0.0625 to 0.0625
- gain_query: float32 [16, 128], P('mp'), may hold values from 0.1 to 1.9
- gain_key: float32 [16, 128], P('mp'), may hold values from 0.1 to 1.9
- gain_attn: float32 [16, 128], replicated, may hold values from 0.1 to 1.9
- gain_mlp: float32 [16, 128], replicated, may hold values from 0.1 to 1.9
Outputs:
- output: bfloat16 [4096, 2048], P('dp')
- grad_tokens: bfloat16 [4096, 2048], P('dp')
- grad_w_query: float32 [2048, 2048], P('dp', 'mp')
- grad_w_key: float32 [2048, 2048], P('dp', 'mp')
- grad_w_value: float32 [2048, 2048], P('dp', 'mp')
- grad_w_output: float32 [2048, 2048], P('mp', 'dp')
- grad_w_gate: float32 [2048, 8192], P('dp', 'mp')
- grad_w_up: float32 [2048, 8192], P('dp', 'mp')
- grad_w_down: float32 [8192, 2048], P('mp', 'dp')
- grad_gain_query: float32 [16, 128], P('mp', 'dp')
- grad_gain_key: float32 [16, 128], P('mp', 'dp')
- grad_gain_attn: float32 [16, 128], P(None, 'dp')
- grad_gain_mlp: float32 [16, 128], P(None, 'dp')
Inputs may be any that keep to these rules, and one draw needn't show every extreme that they name: Index i of dp holds 512 consecutive tokens of row row_ids[i]. Rows 0 and 1 have 1024 tokens, row 2 has 2048, and every block of 512 tokens of every row is held by exactly one index. offsets[i] is the position in its row of the first token of index i; it is a multiple of 512. `doc_ids`: within a row, the document number is 0 at the row's first position and never falls; from one position to the next it rises by 0 or 1. The last position of row 2 has the largest number.
All inputs are finite; a program needn't handle non-finite values.
Results may differ from a plain program's by a relative error of at most 0.025.
Values may be sent and summed in bfloat16 or wider, within the bound.
A program may use at most 192 MiB of HBM per device.

v0:
```python
import math
import jax
import jax.numpy as jnp
from jax import lax
from jax.sharding import PartitionSpec as P

epsilon = 1e-06
rope_base = 500000.0
masked_score = -1e30


def rope_tables(positions, head_width):
    freqs = rope_base ** (-jnp.arange(0, head_width // 2, dtype=jnp.float32) * 2.0 / head_width)
    angles = positions.astype(jnp.float32)[:, None] * freqs[None, :]
    return (jnp.cos(angles)[:, None, :], jnp.sin(angles)[:, None, :])


def rotate(values, cosines, sines):
    half = values.shape[-1] // 2
    first = values[..., :half]
    second = values[..., half:]
    return jnp.concatenate(
        [first * cosines - second * sines, second * cosines + first * sines], axis=-1
    )


def norm_back(grad_normed, normed, factor):
    return factor * (grad_normed - normed * jnp.mean(grad_normed * normed, axis=-1, keepdims=True))


def on_device(
    tokens,
    cotangent,
    doc_ids,
    row_ids,
    offsets,
    w_query,
    w_key,
    w_value,
    w_output,
    w_gate,
    w_up,
    w_down,
    gain_query,
    gain_key,
    gain_attn,
    gain_mlp,
):
    f32 = jnp.float32
    bf16 = jnp.bfloat16
    row_count = tokens.shape[0]
    model_width = tokens.shape[1]
    heads_here = gain_query.shape[0]
    head_width = gain_query.shape[1]
    local_width = heads_here * head_width
    groups = lax.axis_size("dp")
    key_rows = row_count * groups
    block_rows = min(key_rows, row_count * max(1, 512 // row_count))
    block_count = key_rows // block_rows
    score_scale = 1.0 / math.sqrt(head_width)
    positions = offsets[0] + jnp.arange(row_count, dtype=jnp.int32)
    labels = row_ids[0] * key_rows + doc_ids
    cosines, sines = rope_tables(positions, head_width)
    q_raw = jnp.dot(tokens, w_query, preferred_element_type=f32)
    k_raw = jnp.dot(tokens, w_key, preferred_element_type=f32)
    v_raw = jnp.dot(tokens, w_value, preferred_element_type=f32)
    squares = lax.psum(
        jnp.stack([jnp.sum(q_raw * q_raw, axis=1), jnp.sum(k_raw * k_raw, axis=1)]), "mp"
    )
    q_factor = lax.rsqrt(squares[0] / model_width + epsilon)[:, None]
    k_factor = lax.rsqrt(squares[1] / model_width + epsilon)[:, None]
    g_query = gain_query.reshape(local_width)
    g_key = gain_key.reshape(local_width)
    q_normed = q_raw * q_factor
    k_normed = k_raw * k_factor
    queries = rotate(
        (q_normed * g_query).reshape(row_count, heads_here, head_width), cosines, sines
    ).astype(bf16)
    keys_low = rotate(
        (k_normed * g_key).reshape(row_count, heads_here, head_width), cosines, sines
    ).astype(bf16)
    values_low = v_raw.astype(bf16)
    all_keys, all_values, all_labels, all_positions = (
        lax.all_gather(keys_low.reshape(row_count, local_width), "dp", axis=0, tiled=True),
        lax.all_gather(values_low, "dp", axis=0, tiled=True),
        lax.all_gather(labels, "dp", axis=0, tiled=True),
        lax.all_gather(positions, "dp", axis=0, tiled=True),
    )
    key_blocks = all_keys.reshape(block_count, block_rows, heads_here, head_width)
    value_blocks = all_values.reshape(block_count, block_rows, heads_here, head_width)
    label_blocks = all_labels.reshape(block_count, block_rows)
    position_blocks = all_positions.reshape(block_count, block_rows)
    scanned = (key_blocks, value_blocks, label_blocks, position_blocks)
    low_label = jnp.min(labels)
    high_label = jnp.max(labels)

    def scores_of(key_block, label_block, position_block):
        scores = (
            jnp.einsum("qhd,khd->hqk", queries, key_block, preferred_element_type=f32) * score_scale
        )
        allowed = (labels[:, None] == label_block[None, :]) & (
            positions[:, None] >= position_block[None, :]
        )
        return (scores, allowed[None])

    def touches(label_block):
        return (jnp.max(label_block) >= low_label) & (jnp.min(label_block) <= high_label)

    def max_step(carry, blocks_in):
        key_block, value_block, label_block, position_block = blocks_in

        def max_live_block(state):
            running, totals = state
            scores, allowed = scores_of(key_block, label_block, position_block)
            highest = jnp.maximum(
                running, jnp.max(jnp.where(allowed, scores, masked_score), axis=2)
            )
            weights = jnp.where(allowed, jnp.exp(scores - highest[:, :, None]), 0.0)
            return (highest, totals * jnp.exp(running - highest) + jnp.sum(weights, axis=2))

        return (lax.cond(touches(label_block), max_live_block, lambda state: state, carry), None)

    start_state = (
        jnp.full((heads_here, row_count), masked_score, f32),
        jnp.zeros((heads_here, row_count), f32),
    )
    (running_max, running_total), _ = lax.scan(max_step, start_state, scanned)
    log_total = running_max + jnp.log(running_total)

    def value_step(accum, blocks_in):
        key_block, value_block, label_block, position_block = blocks_in

        def value_live_block(current):
            scores, allowed = scores_of(key_block, label_block, position_block)
            probs_low = jnp.where(allowed, jnp.exp(scores - log_total[:, :, None]), 0.0).astype(
                bf16
            )
            return current + jnp.einsum(
                "hqk,khd->qhd", probs_low, value_block, preferred_element_type=f32
            )

        return (
            lax.cond(touches(label_block), value_live_block, lambda current: current, accum),
            None,
        )

    attended, _ = lax.scan(value_step, jnp.zeros((row_count, heads_here, head_width), f32), scanned)
    attended_low = attended.reshape(row_count, local_width).astype(bf16)
    attn_sum = lax.psum(
        jnp.dot(attended_low, w_output, preferred_element_type=f32).astype(jnp.bfloat16), "mp"
    ).astype(jnp.float32)
    attn_factor = lax.rsqrt(jnp.mean(attn_sum * attn_sum, axis=1, keepdims=True) + epsilon)
    attn_normed = attn_sum * attn_factor
    g_attn = gain_attn.reshape(model_width)
    hidden = tokens.astype(f32) + attn_normed * g_attn
    hidden_low = hidden.astype(bf16)
    gate_val = jnp.dot(hidden_low, w_gate, preferred_element_type=f32)
    up_val = jnp.dot(hidden_low, w_up, preferred_element_type=f32)
    sigmoid_gate = jax.nn.sigmoid(gate_val)
    silu_gate = gate_val * sigmoid_gate
    act_low = (silu_gate * up_val).astype(bf16)
    mlp_sum = lax.psum(
        jnp.dot(act_low, w_down, preferred_element_type=f32).astype(jnp.bfloat16), "mp"
    ).astype(jnp.float32)
    mlp_factor = lax.rsqrt(jnp.mean(mlp_sum * mlp_sum, axis=1, keepdims=True) + epsilon)
    mlp_normed = mlp_sum * mlp_factor
    g_mlp = gain_mlp.reshape(model_width)
    output = (hidden + mlp_normed * g_mlp).astype(bf16)
    grad_out = cotangent.astype(f32)
    grad_gain_mlp = jnp.sum(grad_out * mlp_normed, axis=0)
    grad_mlp = norm_back(grad_out * g_mlp, mlp_normed, mlp_factor).astype(bf16)
    grad_w_down = jnp.einsum("tf,td->fd", act_low, grad_mlp, preferred_element_type=f32)
    grad_act = jnp.einsum("td,fd->tf", grad_mlp, w_down, preferred_element_type=f32)
    slope = sigmoid_gate * (1.0 + gate_val * (1.0 - sigmoid_gate))
    grad_gate = (grad_act * up_val * slope).astype(bf16)
    grad_up = (grad_act * silu_gate).astype(bf16)
    branch_grad = jnp.einsum(
        "tf,df->td", grad_gate, w_gate, preferred_element_type=f32
    ) + jnp.einsum("tf,df->td", grad_up, w_up, preferred_element_type=f32)
    grad_hidden = grad_out + lax.psum(branch_grad.astype(jnp.bfloat16), "mp").astype(jnp.float32)
    grad_gain_attn = jnp.sum(grad_hidden * attn_normed, axis=0)
    grad_attn = norm_back(grad_hidden * g_attn, attn_normed, attn_factor).astype(bf16)
    grad_w_output = jnp.einsum("tc,td->cd", attended_low, grad_attn, preferred_element_type=f32)
    grad_attended = (
        jnp.einsum("td,cd->tc", grad_attn, w_output, preferred_element_type=f32)
        .astype(bf16)
        .reshape(row_count, heads_here, head_width)
    )
    delta = jnp.sum(grad_attended.astype(f32) * attended, axis=2).T

    def grad_step(grad_q, blocks_in):
        key_block, value_block, label_block, position_block = blocks_in

        def grad_live_block(current):
            scores, allowed = scores_of(key_block, label_block, position_block)
            probs = jnp.where(allowed, jnp.exp(scores - log_total[:, :, None]), 0.0)
            grad_probs = jnp.einsum(
                "qhd,khd->hqk", grad_attended, value_block, preferred_element_type=f32
            )
            grad_scores = (probs * (grad_probs - delta[:, :, None])).astype(bf16)
            value_term = jnp.einsum(
                "hqk,qhd->khd", probs.astype(bf16), grad_attended, preferred_element_type=f32
            )
            key_term = jnp.einsum("hqk,qhd->khd", grad_scores, queries, preferred_element_type=f32)
            updated = current + jnp.einsum(
                "hqk,khd->qhd", grad_scores, key_block, preferred_element_type=f32
            )
            return (updated, (key_term, value_term))

        def skip_block(current):
            nothing = jnp.zeros((block_rows, heads_here, head_width), f32)
            return (current, (nothing, nothing))

        return lax.cond(touches(label_block), grad_live_block, skip_block, grad_q)

    grad_queries, (key_terms, value_terms) = lax.scan(
        grad_step, jnp.zeros((row_count, heads_here, head_width), f32), scanned
    )
    grad_keys, grad_values = (
        lax.psum_scatter(
            (key_terms.reshape(key_rows, local_width) * score_scale).astype(jnp.bfloat16),
            "dp",
            scatter_dimension=0,
            tiled=True,
        ).astype(jnp.float32),
        lax.psum_scatter(
            value_terms.reshape(key_rows, local_width).astype(jnp.bfloat16),
            "dp",
            scatter_dimension=0,
            tiled=True,
        ).astype(jnp.float32),
    )
    grad_values_low = grad_values.astype(bf16)
    back_q = rotate(grad_queries * score_scale, cosines, -sines).reshape(row_count, local_width)
    back_k = rotate(grad_keys.reshape(row_count, heads_here, head_width), cosines, -sines).reshape(
        row_count, local_width
    )
    grad_gain_query = jnp.sum(back_q * q_normed, axis=0).reshape(heads_here, head_width)
    grad_gain_key = jnp.sum(back_k * k_normed, axis=0).reshape(heads_here, head_width)
    scaled_q = back_q * g_query
    scaled_k = back_k * g_key
    inner = lax.psum(
        jnp.stack([jnp.sum(scaled_q * q_normed, axis=1), jnp.sum(scaled_k * k_normed, axis=1)]),
        "mp",
    )
    grad_q_raw = (q_factor * (scaled_q - q_normed * inner[0][:, None] / model_width)).astype(bf16)
    grad_k_raw = (k_factor * (scaled_k - k_normed * inner[1][:, None] / model_width)).astype(bf16)
    input_term = (
        jnp.einsum("tc,dc->td", grad_q_raw, w_query, preferred_element_type=f32)
        + jnp.einsum("tc,dc->td", grad_k_raw, w_key, preferred_element_type=f32)
        + jnp.einsum("tc,dc->td", grad_values_low, w_value, preferred_element_type=f32)
    )
    grad_tokens = (
        grad_hidden + lax.psum(input_term.astype(jnp.bfloat16), "mp").astype(jnp.float32)
    ).astype(bf16)
    local_w_query = jnp.einsum("td,tc->dc", tokens, grad_q_raw, preferred_element_type=f32)
    local_w_key = jnp.einsum("td,tc->dc", tokens, grad_k_raw, preferred_element_type=f32)
    local_w_value = jnp.einsum("td,tc->dc", tokens, grad_values_low, preferred_element_type=f32)
    local_w_gate = jnp.einsum("td,tf->df", hidden_low, grad_gate, preferred_element_type=f32)
    local_w_up = jnp.einsum("td,tf->df", hidden_low, grad_up, preferred_element_type=f32)
    grad_w_query, grad_w_key, grad_w_value, grad_w_gate, grad_w_up = (
        lax.psum_scatter(
            local_w_query.astype(jnp.bfloat16), "dp", scatter_dimension=0, tiled=True
        ).astype(jnp.float32),
        lax.psum_scatter(
            local_w_key.astype(jnp.bfloat16), "dp", scatter_dimension=0, tiled=True
        ).astype(jnp.float32),
        lax.psum_scatter(
            local_w_value.astype(jnp.bfloat16), "dp", scatter_dimension=0, tiled=True
        ).astype(jnp.float32),
        lax.psum_scatter(
            local_w_gate.astype(jnp.bfloat16), "dp", scatter_dimension=0, tiled=True
        ).astype(jnp.float32),
        lax.psum_scatter(
            local_w_up.astype(jnp.bfloat16), "dp", scatter_dimension=0, tiled=True
        ).astype(jnp.float32),
    )
    summed_out, summed_down, summed_gq, summed_gk, summed_ga, summed_gm = (
        lax.psum_scatter(
            grad_w_output.astype(jnp.bfloat16), "dp", scatter_dimension=1, tiled=True
        ).astype(jnp.float32),
        lax.psum_scatter(
            grad_w_down.astype(jnp.bfloat16), "dp", scatter_dimension=1, tiled=True
        ).astype(jnp.float32),
        lax.psum_scatter(
            grad_gain_query.astype(jnp.bfloat16), "dp", scatter_dimension=1, tiled=True
        ).astype(jnp.float32),
        lax.psum_scatter(
            grad_gain_key.astype(jnp.bfloat16), "dp", scatter_dimension=1, tiled=True
        ).astype(jnp.float32),
        lax.psum_scatter(
            grad_gain_attn.reshape(gain_attn.shape).astype(jnp.bfloat16),
            "dp",
            scatter_dimension=1,
            tiled=True,
        ).astype(jnp.float32),
        lax.psum_scatter(
            grad_gain_mlp.reshape(gain_mlp.shape).astype(jnp.bfloat16),
            "dp",
            scatter_dimension=1,
            tiled=True,
        ).astype(jnp.float32),
    )
    return (
        output,
        grad_tokens,
        grad_w_query,
        grad_w_key,
        grad_w_value,
        summed_out,
        grad_w_gate,
        grad_w_up,
        summed_down,
        summed_gq,
        summed_gk,
        summed_ga,
        summed_gm,
    )


def solution(mesh):
    return jax.shard_map(
        on_device,
        mesh=mesh,
        in_specs=(
            P("dp", None),
            P("dp", None),
            P("dp"),
            P("dp"),
            P("dp"),
            P(None, "mp"),
            P(None, "mp"),
            P(None, "mp"),
            P("mp", None),
            P(None, "mp"),
            P(None, "mp"),
            P("mp", None),
            P("mp", None),
            P("mp", None),
            P(),
            P(),
        ),
        out_specs=(
            P("dp", None),
            P("dp", None),
            P("dp", "mp"),
            P("dp", "mp"),
            P("dp", "mp"),
            P("mp", "dp"),
            P("dp", "mp"),
            P("dp", "mp"),
            P("mp", "dp"),
            P("mp", "dp"),
            P("mp", "dp"),
            P(None, "dp"),
            P(None, "dp"),
        ),
        check_vma=False,
    )
```

profile of v0, /device:TPU:0, one launch (start us, length us, event | category | flops | bytes accessed | tf_op | source)
XLA Modules:
  0.0 1814.4 jit_solution(2751500297274127159)
XLA Ops:
  18.5 8.4 psum.42
  31.7 26.7 %all-gather.1 = s32[8,1,512]{2,1,0:T(1,128)S(1)} all-gather(s32[1,1,512]{2,1,0:T(1,128)S(1)} %bitcast.265), channel_id=1, replica_groups=mesh['dp'=8,'mp'=4] {'dp'}, dimensions={0}, use_global_device_ids=true | all-gather | bytes 18432 | tf_op jit(solution)/shard_map/all_gather | solution.py:87
  59.1 26.6 %all-gather = s32[8,1,512]{2,1,0:T(1,128)S(1)} all-gather(s32[1,1,512]{2,1,0:T(1,128)S(1)} %bitcast.224), channel_id=1, replica_groups=mesh['dp'=8,'mp'=4] {'dp'}, dimensions={0}, use_global_device_ids=true | all-gather | bytes 18432 | tf_op jit(solution)/shard_map/all_gather | solution.py:86
  100.7 63.6 %all-gather.5.cloned.1.call-done = bf16[4096,512]{0,1:T(8,128)(2,1)} async-done(((bf16[512,512]{0,1:T(8,128)(2,1)}), bf16[4096,512]{0,1:T(8,128)(2,1)}) %all-gather.5.cloned.1.call-update) | async-done | bytes 4194320 | tf_op jit(solution)/shard_map/all_gather | solution.py:84
  178.6 33.7 %while.45 = (s32[]{:T(128)}, f32[4,512]{1,0:T(4,128)S(1)}, f32[4,512]{1,0:T(4,128)S(1)}, s32[8,512]{1,0:T(8,128)S(1)}, s32[]{:T(128)}, /*index=5*/s32[]{:T(128)}...) while((s32[]{:T(128)}, f32[4,512]{1,0:T(4,128)S(1)}, ...), condition=%wide.region_12.13_spmd.clone, body=%wide.region_5.12_spmd.clone.sunk | while | flops 276567552 | bytes 10353443 | solution.py:127
  213.4 36.4 %while.46 = (s32[]{:T(128)}, f32[512,4,128]{2,0,1:T(8,128)}, s32[8,512]{1,0:T(8,128)S(1)}, s32[]{:T(128)}, s32[]{:T(128)}, /*index=5*/s32[512]{0:T(512)S(1)}, s3...) while((s32[]{:T(128)}, f32[512,4,128]{2,0,1:T(8,128)}, ...), condition=%wide.region_18.19_spmd.clone, body=%wide.region_13.18_spmd.clone.sunk | while | flops 542115328 | bytes 4226323 | solution.py:147
  256.3 67.2 %all-reduce.5.cloned.1.call-done = bf16[512,2048]{1,0:T(8,128)(2,1)} async-done(((bf16[512,2048]{1,0:T(8,128)(2,1)}), bf16[512,2048]{1,0:T(8,128)(2,1)}) %all-reduce.5.cloned.1.call-update) | async-done | bytes 2097168 | tf_op jit(solution)/shard_map/psum | solution.py:149
  350.7 51.4 %all-reduce.7.cloned.1.call-done = bf16[512,2048]{1,0:T(8,128)(2,1)} async-done(((bf16[512,2048]{1,0:T(8,128)(2,1)}), bf16[512,2048]{1,0:T(8,128)(2,1)}) %all-reduce.7.cloned.1.call-update) | async-done | bytes 2097168 | tf_op jit(solution)/shard_map/psum | solution.py:162
  407.9 11.7 multiply_convert_fusion.1
  427.4 9.4 add_convert_fusion.2
  437.1 51.3 %all-reduce.9.cloned.1.call-done = bf16[512,2048]{1,0:T(8,128)(2,1)} async-done(((bf16[512,2048]{1,0:T(8,128)(2,1)}), bf16[512,2048]{1,0:T(8,128)(2,1)}) %all-reduce.9.cloned.1.call-update) | async-done | bytes 2097168 | tf_op jit(solution)/shard_map/psum | solution.py:180
  506.5 57.7 %while.47 = (s32[]{:T(128)}, f32[512,4,128]{2,0,1:T(8,128)}, f32[8,512,4,128]{3,1,2,0:T(8,128)}, bf16[8,512,4,128]{3,1,2,0:T(8,128)(2,1)}, s32[8,512]{1,0:T(8,12...) while((s32[]{:T(128)}, f32[512,4,128]{2,0,1:T(8,128)}, ...), condition=%wide.region_32.33_spmd.clone, body=%wide.region_27.32_spmd.clone.sunk | while | flops 1353713152 | bytes 40157576 | solution.py:216
  509.9 9.7 conditional.11
  538.7 9.8 conditional.11
  570.8 8.2 copy.77
  585.5 8.0 copy.78
  608.7 84.4 %reduce-scatter.22.cloned.1.call-done = bf16[512,512]{0,1:T(8,128)(2,1)} async-done(((bf16[4096,512]{0,1:T(8,128)(2,1)}), bf16[512,512]{0,1:T(8,128)(2,1)}) %reduce-scatter.22.cloned.1.call-update) | async-done | bytes 524304 | tf_op jit(solution)/shard_map/reduce_scatter | solution.py:220
  719.4 65.5 %reduce-scatter.24.cloned.1.call-done = bf16[512,512]{0,1:T(8,128)(2,1)} async-done(((bf16[4096,512]{0,1:T(8,128)(2,1)}), bf16[512,512]{0,1:T(8,128)(2,1)}) %reduce-scatter.24.cloned.1.call-update) | async-done | bytes 524304 | tf_op jit(solution)/shard_map/reduce_scatter | solution.py:226
  804.8 11.0 convolution_convert_fusion
  816.1 10.0 convolution_convert_fusion.1
  826.2 10.0 convolution_convert_fusion.2
  843.1 54.7 %reduce-scatter.44.cloned.1.call-done = bf16[16,16]{1,0:T(8,128)(2,1)} async-done(((bf16[128,16]{1,0:T(8,128)(2,1)}), bf16[16,16]{1,0:T(8,128)(2,1)}) %reduce-scatter.44.cloned.1.call-update) | async-done | bytes 528
  899.2 70.4 %reduce-scatter.32.cloned.1.call-done = bf16[512,256]{1,0:T(8,128)(2,1)} async-done(((bf16[512,2048]{1,0:T(8,128)(2,1)}), bf16[512,256]{1,0:T(8,128)(2,1)}) %reduce-scatter.32.cloned.1.call-update) | async-done | bytes 262160 | tf_op jit(solution)/shard_map/reduce_scatter | solution.py:279
  971.4 54.8 %reduce-scatter.42.cloned.1.call-done = bf16[16,4]{1,0:T(8,128)(2,1)} async-done(((bf16[128,4]{1,0:T(8,128)(2,1)}), bf16[16,4]{1,0:T(8,128)(2,1)}) %reduce-scatter.42.cloned.1.call-update) | async-done | bytes 144
  1027.5 55.1 %reduce-scatter.40.cloned.1.call-done = bf16[16,4]{1,0:T(8,128)(2,1)} async-done(((bf16[128,4]{1,0:T(8,128)(2,1)}), bf16[16,4]{1,0:T(8,128)(2,1)}) %reduce-scatter.40.cloned.1.call-update) | async-done | bytes 144
  1084.0 52.2 %all-reduce.11.cloned.1.call-done = bf16[512,2048]{1,0:T(8,128)(2,1)} async-done(((bf16[512,2048]{1,0:T(8,128)(2,1)}), bf16[512,2048]{1,0:T(8,128)(2,1)}) %all-reduce.11.cloned.1.call-update) | async-done | bytes 2097168 | tf_op jit(solution)/shard_map/psum | solution.py:254
  1141.8 65.9 %reduce-scatter.30.cloned.1.call-done = bf16[256,512]{0,1:T(8,128)(2,1)} async-done(((bf16[2048,512]{0,1:T(8,128)(2,1)}), bf16[256,512]{0,1:T(8,128)(2,1)}) %reduce-scatter.30.cloned.1.call-update) | async-done | bytes 262160 | tf_op jit(solution)/shard_map/reduce_scatter | solution.py:268
  1209.6 69.1 %reduce-scatter.26.cloned.1.call-done = bf16[256,512]{0,1:T(8,128)(2,1)} async-done(((bf16[2048,512]{0,1:T(8,128)(2,1)}), bf16[256,512]{0,1:T(8,128)(2,1)}) %reduce-scatter.26.cloned.1.call-update) | async-done | bytes 262160 | tf_op jit(solution)/shard_map/reduce_scatter | solution.py:262
  1280.6 68.8 %reduce-scatter.28.cloned.1.call-done = bf16[256,512]{0,1:T(8,128)(2,1)} async-done(((bf16[2048,512]{0,1:T(8,128)(2,1)}), bf16[256,512]{0,1:T(8,128)(2,1)}) %reduce-scatter.28.cloned.1.call-update) | async-done | bytes 262160 | tf_op jit(solution)/shard_map/reduce_scatter | solution.py:265
  1351.2 150.0 %reduce-scatter.38.cloned.1.call-done = bf16[2048,256]{1,0:T(8,128)(2,1)} async-done(((bf16[2048,2048]{1,0:T(8,128)(2,1)}), bf16[2048,256]{1,0:T(8,128)(2,1)}) %reduce-scatter.38.cloned.1.call-update) | async-done | bytes 1048592 | tf_op jit(solution)/shard_map/reduce_scatter | solution.py:282
  1503.9 149.3 %reduce-scatter.36.cloned.1.call-done = bf16[256,2048]{1,0:T(8,128)(2,1)} async-done(((bf16[2048,2048]{1,0:T(8,128)(2,1)}), bf16[256,2048]{1,0:T(8,128)(2,1)}) %reduce-scatter.36.cloned.1.call-update) | async-done | bytes 1048592 | tf_op jit(solution)/shard_map/reduce_scatter | solution.py:274
  1656.0 148.9 %reduce-scatter.34.cloned.1.call-done = bf16[256,2048]{1,0:T(8,128)(2,1)} async-done(((bf16[2048,2048]{1,0:T(8,128)(2,1)}), bf16[256,2048]{1,0:T(8,128)(2,1)}) %reduce-scatter.34.cloned.1.call-update) | async-done | bytes 1048592 | tf_op jit(solution)/shard_map/reduce_scatter | solution.py:271
  (354 shorter events, 301.7 us)
Async XLA Ops:
  7.2 8.9 copy-start
  7.2 81.1 %all-gather.7.cloned.1.call-start = ((), (), s32[]{:S(2)}) async-start(), calls=%async_computation.14 | async-start | bytes 4718592 | tf_op jit(solution)/shard_map/all_gather | solution.py:85
  11.7 152.6 %all-gather.5.cloned.1.call-start = ((), (), s32[]{:S(2)}) async-start(), calls=%async_computation.13 | async-start | bytes 4718592 | tf_op jit(solution)/shard_map/all_gather | solution.py:84
  16.1 13.5 copy-start.9
  16.1 12.0 copy-start.30
  16.1 13.4 copy-start.32
  28.1 30.3 %copy-start.34 = (s32[512]{0:T(512)S(1)}, s32[512]{0:T(512)}, u32[]{:S(2)}) copy-start(s32[512]{0:T(512)} %param.30) | copy-start | bytes 6148
  31.0 292.5 %all-reduce.5.cloned.1.call-start = ((), (), s32[]{:S(2)}) async-start(), calls=%async_computation.15 | async-start | bytes 4194304 | tf_op jit(solution)/shard_map/psum | solution.py:149
  251.3 74.2 %copy-start.21 = (bf16[512,4,128]{0,2,1:T(8,128)(2,1)}, bf16[512,4,128]{0,2,1:T(8,128)(2,1)S(1)}, u32[]{:S(2)}) copy-start(bf16[512,4,128]{0,2,1:T(8,128)(2,1)S(1)} %copy.70) | copy-start | bytes 1572868
  251.3 74.3 %copy-start.24 = (f32[16,128]{1,0:T(8,128)S(1)}, f32[16,128]{1,0:T(8,128)}, u32[]{:S(2)}) copy-start(f32[16,128]{1,0:T(8,128)} %param.42) | copy-start | bytes 24580
  255.8 146.3 %all-reduce.7.cloned.1.call-start = ((), (), s32[]{:S(2)}) async-start(), calls=%async_computation.16 | async-start | bytes 4194304 | tf_op jit(solution)/shard_map/psum | solution.py:162
  325.6 11.2 slice-start.2
  329.1 15.6 slice-start
  336.9 7.8 slice-start.1
  350.4 53.9 %copy-start.25 = (f32[16,128]{1,0:T(8,128)S(1)}, f32[16,128]{1,0:T(8,128)}, u32[]{:S(2)}) copy-start(f32[16,128]{1,0:T(8,128)} %param.43) | copy-start | bytes 24580
  350.5 138.0 %all-reduce.9.cloned.1.call-start = ((), (), s32[]{:S(2)}) async-start(), calls=%async_computation.17 | async-start | bytes 4194304 | tf_op jit(solution)/shard_map/psum | solution.py:180
  436.8 256.3 %reduce-scatter.22.cloned.1.call-start = ((), (), s32[]{:S(2)}) async-start(), calls=%async_computation.18 | async-start | bytes 4718592 | tf_op jit(solution)/shard_map/reduce_scatter | solution.py:220
  585.5 199.5 %reduce-scatter.24.cloned.1.call-start = ((), (), s32[]{:S(2)}) async-start(), calls=%async_computation.19 | async-start | bytes 4718592 | tf_op jit(solution)/shard_map/reduce_scatter | solution.py:226
  599.9 241.9 %reduce-scatter.46.cloned.1.call-start = ((), (), s32[]{:S(2)}) async-start(), calls=%async_computation.31 | async-start | bytes 36864
  600.7 297.1 %reduce-scatter.44.cloned.1.call-start = ((), (), s32[]{:S(2)}) async-start(), calls=%async_computation.30 | async-start | bytes 36864
  601.5 368.1 %reduce-scatter.32.cloned.1.call-start = ((), (), s32[]{:S(2)}) async-start(), calls=%async_computation.24 | async-start | bytes 2359296 | tf_op jit(solution)/shard_map/reduce_scatter | solution.py:279
  605.9 88.3 %copy-start.20 = (f32[512,64]{0,1:T(8,128)S(1)}, f32[512,64]{0,1:T(8,128)}, u32[]{:S(2)}) copy-start(f32[512,64]{0,1:T(8,128)} %copy-done.19) | copy-start | bytes 393220
  605.9 88.3 %copy-start.23 = (f32[512,64]{0,1:T(8,128)S(1)}, f32[512,64]{0,1:T(8,128)}, u32[]{:S(2)}) copy-start(f32[512,64]{0,1:T(8,128)} %get-tuple-element.872) | copy-start | bytes 393220
  606.0 420.2 %reduce-scatter.42.cloned.1.call-start = ((), (), s32[]{:S(2)}) async-start(), calls=%async_computation.29 | async-start | bytes 36864
  713.5 369.2 %reduce-scatter.40.cloned.1.call-start = ((), (), s32[]{:S(2)}) async-start(), calls=%async_computation.28 | async-start | bytes 36864
  719.2 417.0 %all-reduce.11.cloned.1.call-start = ((), (), s32[]{:S(2)}) async-start(), calls=%async_computation.20 | async-start | bytes 4194304 | tf_op jit(solution)/shard_map/psum | solution.py:254
  791.9 415.8 %reduce-scatter.30.cloned.1.call-start = ((), (), s32[]{:S(2)}) async-start(), calls=%async_computation.23 | async-start | bytes 2359296 | tf_op jit(solution)/shard_map/reduce_scatter | solution.py:268
  796.2 482.5 %reduce-scatter.26.cloned.1.call-start = ((), (), s32[]{:S(2)}) async-start(), calls=%async_computation.21 | async-start | bytes 2359296 | tf_op jit(solution)/shard_map/reduce_scatter | solution.py:262
  800.5 548.9 %reduce-scatter.28.cloned.1.call-start = ((), (), s32[]{:S(2)}) async-start(), calls=%async_computation.22 | async-start | bytes 2359296 | tf_op jit(solution)/shard_map/reduce_scatter | solution.py:265
  804.8 696.5 %reduce-scatter.38.cloned.1.call-start = ((), (), s32[]{:S(2)}) async-start(), calls=%async_computation.27 | async-start | bytes 9437184 | tf_op jit(solution)/shard_map/reduce_scatter | solution.py:282
  815.8 837.4 %reduce-scatter.36.cloned.1.call-start = ((), (), s32[]{:S(2)}) async-start(), calls=%async_computation.26 | async-start | bytes 9437184 | tf_op jit(solution)/shard_map/reduce_scatter | solution.py:274
  826.1 978.7 %reduce-scatter.34.cloned.1.call-start = ((), (), s32[]{:S(2)}) async-start(), calls=%async_computation.25 | async-start | bytes 9437184 | tf_op jit(solution)/shard_map/reduce_scatter | solution.py:271
  (33 other events, 128.8 us)
Sparse Core Ops, SparseCore 0:
  11.8 76.4 all-gather.6
  90.9 73.3 all-gather.4
  255.9 67.5 all-reduce.4
  350.6 51.4 all-reduce.6
  436.9 51.4 all-reduce.8
  585.6 107.4 reduce-scatter.21
  696.7 88.2 reduce-scatter.23
  788.4 53.3 reduce-scatter.45
  845.2 52.5 reduce-scatter.43
  902.2 67.3 reduce-scatter.31
  973.6 52.4 reduce-scatter.41
  1030.0 52.5 reduce-scatter.39
  1085.7 50.4 all-reduce.10
  1139.6 68.0 reduce-scatter.29
  1211.6 67.0 reduce-scatter.25
  1282.1 67.2 reduce-scatter.27
  1352.8 148.3 reduce-scatter.37
  1505.1 148.0 reduce-scatter.35
  1656.8 148.0 reduce-scatter.33
where the time goes:
time: 1820 us; the launch traced here: 1810 us
  waiting for transfers between devices  1330 us (73%)
  matrix products  157 us (9%)
  local copies, waits for them, and re-layouts  89.8 us (5%)
  other arithmetic  86.4 us (5%)
  blocking collectives  68.6 us (4%)
  loops' own time  63.2 us (3%)
    unnamed x23, waiting for transfers between devices  170 us
    reduce_scatter x1, waiting for transfers between devices, on_device(): lax.psum_scatter(grad_w_down.astype(jnp.bfloat16), 'dp', scatter_dimensio...  150 us
    reduce_scatter x1, waiting for transfers between devices, on_device(): lax.psum_scatter(local_w_up.astype(jnp.bfloat16), 'dp', scatter_dimension...  149 us
    reduce_scatter x1, waiting for transfers between devices, on_device(): lax.psum_scatter(local_w_gate.astype(jnp.bfloat16), 'dp', scatter_dimensi...  149 us
    reduce_scatter x1, waiting for transfers between devices, on_device(): lax.psum_scatter((key_terms.reshape(key_rows, local_width) * score_scale)...  84.4 us
    reduce_scatter x1, waiting for transfers between devices, on_device(): lax.psum_scatter(grad_w_output.astype(jnp.bfloat16), 'dp', scatter_dimens...  70.4 us
    reduce_scatter x1, waiting for transfers between devices, on_device(): lax.psum_scatter(local_w_query.astype(jnp.bfloat16), 'dp', scatter_dimens...  69.1 us
    reduce_scatter x1, waiting for transfers between devices, on_device(): lax.psum_scatter(local_w_key.astype(jnp.bfloat16), 'dp', scatter_dimensio...  68.8 us
  transfers between devices with their start and end apart: 19, of which 19 were waited for; matrix products, arithmetic and copies ran while one was open for 8% of the time, Pallas kernels for 0%

commit v1 on v0

--- a/solution.py
+++ b/solution.py
@@ -251,7 +251,8 @@
         + jnp.einsum("tc,dc->td", grad_values_low, w_value, preferred_element_type=f32)
     )
     grad_tokens = (
-        grad_hidden + lax.psum(input_term.astype(jnp.bfloat16), "mp").astype(jnp.float32)
+        grad_hidden
+        + jnp.sum(lax.all_gather(input_term.astype(jnp.bfloat16), "mp"), axis=0).astype(jnp.float32)
     ).astype(bf16)
     local_w_query = jnp.einsum("td,tc->dc", tokens, grad_q_raw, preferred_element_type=f32)
     local_w_key = jnp.einsum("td,tc->dc", tokens, grad_k_raw, preferred_element_type=f32)

time: 1820 us -> 1840 us (1.011)
    all_gather x0 -> x1, waiting for transfers between devices: none -> 56.7 us  [on_device(): lax.all_gather(input_term.astype(jnp.bfloat16), 'mp')]
    psum x1 -> x0, waiting for transfers between devices: 52.2 us -> none  [on_device(): lax.psum(input_term.astype(jnp.bfloat16), 'mp').astype(jnp.float32)]
    unnamed x104 -> x108, local copies, waits for them, and re-layouts: 49.4 us -> 52.9 us
  transfers between devices with their start and end apart: 19 -> 19, of which waited for: 19 -> 18; matrix products, arithmetic and copies ran while one was open for 8% -> 7% of each run, Pallas kernels for 0% -> 0%
where the time goes in v1:
time: 1840 us; the launch traced here: 1830 us
  waiting for transfers between devices  1340 us (73%)
  matrix products  148 us (8%)
  other arithmetic  96.1 us (5%)
  local copies, waits for them, and re-layouts  93.3 us (5%)
  blocking collectives  68.5 us (4%)
  loops' own time  60.8 us (3%)
    unnamed x23, waiting for transfers between devices  158 us
    reduce_scatter x1, waiting for transfers between devices, on_device(): lax.psum_scatter(grad_w_down.astype(jnp.bfloat16), 'dp', scatter_dimensio...  150 us
    reduce_scatter x1, waiting for transfers between devices, on_device(): lax.psum_scatter(local_w_gate.astype(jnp.bfloat16), 'dp', scatter_dimensi...  149 us
    reduce_scatter x1, waiting for transfers between devices, on_device(): lax.psum_scatter(local_w_up.astype(jnp.bfloat16), 'dp', scatter_dimension...  149 us
    reduce_scatter x1, waiting for transfers between devices, on_device(): lax.psum_scatter((key_terms.reshape(key_rows, local_width) * score_scale)...  83.5 us
    reduce_scatter x1, waiting for transfers between devices, on_device(): lax.psum_scatter(value_terms.reshape(key_rows, local_width).astype(jnp.bf...  82.9 us
    reduce_scatter x1, waiting for transfers between devices, on_device(): lax.psum_scatter(local_w_key.astype(jnp.bfloat16), 'dp', scatter_dimensio...  70 us
    reduce_scatter x1, waiting for transfers between devices, on_device(): lax.psum_scatter(grad_w_output.astype(jnp.bfloat16), 'dp', scatter_dimens...  69.8 us
  transfers between devices with their start and end apart: 19, of which 18 were waited for; matrix products, arithmetic and copies ran while one was open for 7% of the time, Pallas kernels for 0%

profile of v1, /device:TPU:0, one launch (start us, length us, event | category | flops | bytes accessed | tf_op | source)
XLA Modules:
  0.0 1828.4 jit_solution(26648415566499872)
XLA Ops:
  18.5 8.4 psum.35
  32.4 26.6 %all-gather.2 = s32[8,1,512]{2,1,0:T(1,128)S(1)} all-gather(s32[1,1,512]{2,1,0:T(1,128)S(1)} %bitcast.267), channel_id=1, replica_groups=mesh['dp'=8,'mp'=4] {'dp'}, dimensions={0}, use_global_device_ids=true | all-gather | bytes 18432 | tf_op jit(solution)/shard_map/all_gather | solution.py:87
  59.7 26.6 %all-gather.1 = s32[8,1,512]{2,1,0:T(1,128)S(1)} all-gather(s32[1,1,512]{2,1,0:T(1,128)S(1)} %bitcast.226), channel_id=1, replica_groups=mesh['dp'=8,'mp'=4] {'dp'}, dimensions={0}, use_global_device_ids=true | all-gather | bytes 18432 | tf_op jit(solution)/shard_map/all_gather | solution.py:86
  100.6 63.7 %all-gather.7.cloned.1.call-done = bf16[4096,512]{0,1:T(8,128)(2,1)} async-done(((bf16[512,512]{0,1:T(8,128)(2,1)}), bf16[4096,512]{0,1:T(8,128)(2,1)}) %all-gather.7.cloned.1.call-update) | async-done | bytes 4194320 | tf_op jit(solution)/shard_map/all_gather | solution.py:84
  178.7 33.1 %while.45 = (s32[]{:T(128)}, f32[4,512]{1,0:T(4,128)S(1)}, f32[4,512]{1,0:T(4,128)S(1)}, s32[8,512]{1,0:T(8,128)S(1)}, s32[]{:T(128)}, /*index=5*/s32[]{:T(128)}...) while((s32[]{:T(128)}, f32[4,512]{1,0:T(4,128)S(1)}, ...), condition=%wide.region_12.13_spmd.clone, body=%wide.region_5.12_spmd.clone.sunk | while | flops 276567552 | bytes 10353443 | solution.py:127
  212.8 35.8 %while.46 = (s32[]{:T(128)}, f32[512,4,128]{2,0,1:T(8,128)}, s32[8,512]{1,0:T(8,128)S(1)}, s32[]{:T(128)}, s32[]{:T(128)}, /*index=5*/s32[512]{0:T(512)S(1)}, s3...) while((s32[]{:T(128)}, f32[512,4,128]{2,0,1:T(8,128)}, ...), condition=%wide.region_18.19_spmd.clone, body=%wide.region_13.18_spmd.clone.sunk | while | flops 542115328 | bytes 4226323 | solution.py:147
  255.0 67.2 %all-reduce.4.cloned.1.call-done = bf16[512,2048]{1,0:T(8,128)(2,1)} async-done(((bf16[512,2048]{1,0:T(8,128)(2,1)}), bf16[512,2048]{1,0:T(8,128)(2,1)}) %all-reduce.4.cloned.1.call-update) | async-done | bytes 2097168 | tf_op jit(solution)/shard_map/psum | solution.py:149
  349.3 51.4 %all-reduce.6.cloned.1.call-done = bf16[512,2048]{1,0:T(8,128)(2,1)} async-done(((bf16[512,2048]{1,0:T(8,128)(2,1)}), bf16[512,2048]{1,0:T(8,128)(2,1)}) %all-reduce.6.cloned.1.call-update) | async-done | bytes 2097168 | tf_op jit(solution)/shard_map/psum | solution.py:162
  406.5 11.7 multiply_convert_fusion.1
  426.0 9.4 add_convert_fusion.2
  435.7 51.3 %all-reduce.8.cloned.1.call-done = bf16[512,2048]{1,0:T(8,128)(2,1)} async-done(((bf16[512,2048]{1,0:T(8,128)(2,1)}), bf16[512,2048]{1,0:T(8,128)(2,1)}) %all-reduce.8.cloned.1.call-update) | async-done | bytes 2097168 | tf_op jit(solution)/shard_map/psum | solution.py:180
  505.1 56.1 %while.47 = (s32[]{:T(128)}, f32[512,4,128]{2,0,1:T(8,128)}, f32[8,512,4,128]{3,1,2,0:T(8,128)}, bf16[8,512,4,128]{3,1,2,0:T(8,128)(2,1)}, s32[8,512]{1,0:T(8,12...) while((s32[]{:T(128)}, f32[512,4,128]{2,0,1:T(8,128)}, ...), condition=%wide.region_32.33_spmd.clone, body=%wide.region_27.32_spmd.clone.sunk | while | flops 1353713152 | bytes 40157576 | solution.py:216
  508.2 9.8 conditional.11
  536.3 9.8 conditional.11
  567.7 8.2 copy.77
  582.4 8.0 copy.78
  606.6 83.5 %reduce-scatter.22.cloned.1.call-done = bf16[512,512]{0,1:T(8,128)(2,1)} async-done(((bf16[4096,512]{0,1:T(8,128)(2,1)}), bf16[512,512]{0,1:T(8,128)(2,1)}) %reduce-scatter.22.cloned.1.call-update) | async-done | bytes 524304 | tf_op jit(solution)/shard_map/reduce_scatter | solution.py:220
  699.0 82.9 %reduce-scatter.24.cloned.1.call-done = bf16[512,512]{0,1:T(8,128)(2,1)} async-done(((bf16[4096,512]{0,1:T(8,128)(2,1)}), bf16[512,512]{0,1:T(8,128)(2,1)}) %reduce-scatter.24.cloned.1.call-update) | async-done | bytes 524304 | tf_op jit(solution)/shard_map/reduce_scatter | solution.py:226
  806.7 11.0 convolution_convert_fusion
  817.8 10.0 convolution_convert_fusion.1
  828.1 10.0 convolution_convert_fusion.2
  846.5 48.2 %reduce-scatter.44.cloned.1.call-done = bf16[16,16]{1,0:T(8,128)(2,1)} async-done(((bf16[128,16]{1,0:T(8,128)(2,1)}), bf16[16,16]{1,0:T(8,128)(2,1)}) %reduce-scatter.44.cloned.1.call-update) | async-done | bytes 528
  896.0 69.8 %reduce-scatter.32.cloned.1.call-done = bf16[512,256]{1,0:T(8,128)(2,1)} async-done(((bf16[512,2048]{1,0:T(8,128)(2,1)}), bf16[512,256]{1,0:T(8,128)(2,1)}) %reduce-scatter.32.cloned.1.call-update) | async-done | bytes 262160 | tf_op jit(solution)/shard_map/reduce_scatter | solution.py:280
  967.6 54.8 %reduce-scatter.42.cloned.1.call-done = bf16[16,4]{1,0:T(8,128)(2,1)} async-done(((bf16[128,4]{1,0:T(8,128)(2,1)}), bf16[16,4]{1,0:T(8,128)(2,1)}) %reduce-scatter.42.cloned.1.call-update) | async-done | bytes 144
  1023.8 55.1 %reduce-scatter.40.cloned.1.call-done = bf16[16,4]{1,0:T(8,128)(2,1)} async-done(((bf16[128,4]{1,0:T(8,128)(2,1)}), bf16[16,4]{1,0:T(8,128)(2,1)}) %reduce-scatter.40.cloned.1.call-update) | async-done | bytes 144
  1080.2 69.8 %reduce-scatter.30.cloned.1.call-done = bf16[256,512]{0,1:T(8,128)(2,1)} async-done(((bf16[2048,512]{0,1:T(8,128)(2,1)}), bf16[256,512]{0,1:T(8,128)(2,1)}) %reduce-scatter.30.cloned.1.call-update) | async-done | bytes 262160 | tf_op jit(solution)/shard_map/reduce_scatter | solution.py:269
  1151.9 69.8 %reduce-scatter.26.cloned.1.call-done = bf16[256,512]{0,1:T(8,128)(2,1)} async-done(((bf16[2048,512]{0,1:T(8,128)(2,1)}), bf16[256,512]{0,1:T(8,128)(2,1)}) %reduce-scatter.26.cloned.1.call-update) | async-done | bytes 262160 | tf_op jit(solution)/shard_map/reduce_scatter | solution.py:263
  1223.6 70.0 %reduce-scatter.28.cloned.1.call-done = bf16[256,512]{0,1:T(8,128)(2,1)} async-done(((bf16[2048,512]{0,1:T(8,128)(2,1)}), bf16[256,512]{0,1:T(8,128)(2,1)}) %reduce-scatter.28.cloned.1.call-update) | async-done | bytes 262160 | tf_op jit(solution)/shard_map/reduce_scatter | solution.py:266
  1295.5 150.5 %reduce-scatter.38.cloned.1.call-done = bf16[2048,256]{1,0:T(8,128)(2,1)} async-done(((bf16[2048,2048]{1,0:T(8,128)(2,1)}), bf16[2048,256]{1,0:T(8,128)(2,1)}) %reduce-scatter.38.cloned.1.call-update) | async-done | bytes 1048592 | tf_op jit(solution)/shard_map/reduce_scatter | solution.py:283
  1448.6 148.8 %reduce-scatter.36.cloned.1.call-done = bf16[256,2048]{1,0:T(8,128)(2,1)} async-done(((bf16[2048,2048]{1,0:T(8,128)(2,1)}), bf16[256,2048]{1,0:T(8,128)(2,1)}) %reduce-scatter.36.cloned.1.call-update) | async-done | bytes 1048592 | tf_op jit(solution)/shard_map/reduce_scatter | solution.py:275
  1600.2 149.2 %reduce-scatter.34.cloned.1.call-done = bf16[256,2048]{1,0:T(8,128)(2,1)} async-done(((bf16[2048,2048]{1,0:T(8,128)(2,1)}), bf16[256,2048]{1,0:T(8,128)(2,1)}) %reduce-scatter.34.cloned.1.call-update) | async-done | bytes 1048592 | tf_op jit(solution)/shard_map/reduce_scatter | solution.py:272
  1752.2 56.7 %all-gather.11.cloned.1.call-done = bf16[2048,2048]{1,0:T(8,128)(2,1)} async-done(((bf16[512,2048]{1,0:T(8,128)(2,1)}), bf16[2048,2048]{1,0:T(8,128)(2,1)}) %all-gather.11.cloned.1.call-update) | async-done | bytes 8388624 | tf_op jit(solution)/shard_map/all_gather | solution.py:255
  (359 shorter events, 298.2 us)
Async XLA Ops:
  7.2 9.9 copy-start
  7.2 81.1 %all-gather.9.cloned.1.call-start = ((), (), s32[]{:S(2)}) async-start(), calls=%async_computation.14 | async-start | bytes 4718592 | tf_op jit(solution)/shard_map/all_gather | solution.py:85
  11.7 152.7 %all-gather.7.cloned.1.call-start = ((), (), s32[]{:S(2)}) async-start(), calls=%async_computation.13 | async-start | bytes 4718592 | tf_op jit(solution)/shard_map/all_gather | solution.py:84
  17.1 11.0 copy-start.34
  17.1 11.2 copy-start.32
  18.5 13.2 copy-start.9
  28.1 30.9 %copy-start.36 = (s32[512]{0:T(512)S(1)}, s32[512]{0:T(512)}, u32[]{:S(2)}) copy-start(s32[512]{0:T(512)} %param.30) | copy-start | bytes 6148
  31.7 290.5 %all-reduce.4.cloned.1.call-start = ((), (), s32[]{:S(2)}) async-start(), calls=%async_computation.15 | async-start | bytes 4194304 | tf_op jit(solution)/shard_map/psum | solution.py:149
  250.0 74.2 %copy-start.23 = (bf16[512,4,128]{0,2,1:T(8,128)(2,1)}, bf16[512,4,128]{0,2,1:T(8,128)(2,1)S(1)}, u32[]{:S(2)}) copy-start(bf16[512,4,128]{0,2,1:T(8,128)(2,1)S(1)} %copy.70) | copy-start | bytes 1572868
  250.0 74.2 %copy-start.26 = (f32[16,128]{1,0:T(8,128)S(1)}, f32[16,128]{1,0:T(8,128)}, u32[]{:S(2)}) copy-start(f32[16,128]{1,0:T(8,128)} %param.42) | copy-start | bytes 24580
  254.4 146.3 %all-reduce.6.cloned.1.call-start = ((), (), s32[]{:S(2)}) async-start(), calls=%async_computation.16 | async-start | bytes 4194304 | tf_op jit(solution)/shard_map/psum | solution.py:162
  324.2 11.2 slice-start.2
  327.7 15.6 slice-start
  335.5 7.8 slice-start.1
  349.0 53.9 %copy-start.27 = (f32[16,128]{1,0:T(8,128)S(1)}, f32[16,128]{1,0:T(8,128)}, u32[]{:S(2)}) copy-start(f32[16,128]{1,0:T(8,128)} %param.43) | copy-start | bytes 24580
  349.1 138.0 %all-reduce.8.cloned.1.call-start = ((), (), s32[]{:S(2)}) async-start(), calls=%async_computation.17 | async-start | bytes 4194304 | tf_op jit(solution)/shard_map/psum | solution.py:180
  435.4 254.7 %reduce-scatter.22.cloned.1.call-start = ((), (), s32[]{:S(2)}) async-start(), calls=%async_computation.18 | async-start | bytes 4718592 | tf_op jit(solution)/shard_map/reduce_scatter | solution.py:220
  582.4 199.5 %reduce-scatter.24.cloned.1.call-start = ((), (), s32[]{:S(2)}) async-start(), calls=%async_computation.19 | async-start | bytes 4718592 | tf_op jit(solution)/shard_map/reduce_scatter | solution.py:226
  596.8 248.3 %reduce-scatter.46.cloned.1.call-start = ((), (), s32[]{:S(2)}) async-start(), calls=%async_computation.31 | async-start | bytes 36864
  597.6 297.0 %reduce-scatter.44.cloned.1.call-start = ((), (), s32[]{:S(2)}) async-start(), calls=%async_computation.30 | async-start | bytes 36864
  598.4 367.4 %reduce-scatter.32.cloned.1.call-start = ((), (), s32[]{:S(2)}) async-start(), calls=%async_computation.23 | async-start | bytes 2359296 | tf_op jit(solution)/shard_map/reduce_scatter | solution.py:280
  602.9 88.4 %copy-start.22 = (f32[512,64]{0,1:T(8,128)S(1)}, f32[512,64]{0,1:T(8,128)}, u32[]{:S(2)}) copy-start(f32[512,64]{0,1:T(8,128)} %copy-done.21) | copy-start | bytes 393220
  602.9 88.4 %copy-start.25 = (f32[512,64]{0,1:T(8,128)S(1)}, f32[512,64]{0,1:T(8,128)}, u32[]{:S(2)}) copy-start(f32[512,64]{0,1:T(8,128)} %get-tuple-element.872) | copy-start | bytes 393220
  603.0 419.5 %reduce-scatter.42.cloned.1.call-start = ((), (), s32[]{:S(2)}) async-start(), calls=%async_computation.29 | async-start | bytes 36864
  696.3 382.6 %reduce-scatter.40.cloned.1.call-start = ((), (), s32[]{:S(2)}) async-start(), calls=%async_computation.28 | async-start | bytes 36864
  699.0 451.1 %reduce-scatter.30.cloned.1.call-start = ((), (), s32[]{:S(2)}) async-start(), calls=%async_computation.22 | async-start | bytes 2359296 | tf_op jit(solution)/shard_map/reduce_scatter | solution.py:269
  786.2 435.5 %reduce-scatter.26.cloned.1.call-start = ((), (), s32[]{:S(2)}) async-start(), calls=%async_computation.20 | async-start | bytes 2359296 | tf_op jit(solution)/shard_map/reduce_scatter | solution.py:263
  800.0 493.6 %reduce-scatter.28.cloned.1.call-start = ((), (), s32[]{:S(2)}) async-start(), calls=%async_computation.21 | async-start | bytes 2359296 | tf_op jit(solution)/shard_map/reduce_scatter | solution.py:266
  806.7 639.3 %reduce-scatter.38.cloned.1.call-start = ((), (), s32[]{:S(2)}) async-start(), calls=%async_computation.26 | async-start | bytes 9437184 | tf_op jit(solution)/shard_map/reduce_scatter | solution.py:283
  817.7 779.7 %reduce-scatter.36.cloned.1.call-start = ((), (), s32[]{:S(2)}) async-start(), calls=%async_computation.25 | async-start | bytes 9437184 | tf_op jit(solution)/shard_map/reduce_scatter | solution.py:275
  827.8 921.6 %reduce-scatter.34.cloned.1.call-start = ((), (), s32[]{:S(2)}) async-start(), calls=%async_computation.24 | async-start | bytes 9437184 | tf_op jit(solution)/shard_map/reduce_scatter | solution.py:272
  838.1 970.7 %all-gather.11.cloned.1.call-start = ((), (), s32[]{:S(2)}) async-start(), calls=%async_computation.27 | async-start | bytes 10485760 | tf_op jit(solution)/shard_map/all_gather | solution.py:255
  (35 other events, 124.5 us)
Sparse Core Ops, SparseCore 0:
  11.8 76.4 all-gather.8
  90.9 73.4 all-gather.6
  254.5 67.5 all-reduce.3
  349.2 51.4 all-reduce.5
  435.6 51.4 all-reduce.7
  582.5 107.6 reduce-scatter.21
  693.8 88.0 reduce-scatter.23
  785.3 53.2 reduce-scatter.45
  842.1 52.5 reduce-scatter.43
  898.4 67.3 reduce-scatter.31
  969.8 52.5 reduce-scatter.41
  1026.3 52.5 reduce-scatter.39
  1082.8 67.1 reduce-scatter.29
  1154.4 67.2 reduce-scatter.25
  1226.1 67.4 reduce-scatter.27
  1297.5 148.3 reduce-scatter.37
  1449.4 147.9 reduce-scatter.35
  1601.4 148.0 reduce-scatter.33
  1751.5 57.2 all-gather.10
